TPU v7x, 128 devices: a whole 4x4x4 slice. The times are simulated.
128 devices in a mesh: variant: 8 (over z_lo, x), vocab: 16 (over y, z_hi, core).
Axes of the slice: x: 4, y: 4, z: 4 (z_hi: 2, z_lo: 2; z = z_hi * 2 + z_lo), core: 2. Of those that a mesh axis runs over, the one named last changes fastest.
Arguments:
- teacher_hidden: bfloat16 [8, 256, 4096], P(None, None, ('variant', 'vocab')), may hold values from -24 to 24
- teacher_weight: bfloat16 [4096, 64128], P(None, ('vocab', 'variant')), may hold values from -1 to 1
- variant_ids: int32 [8], replicated, may hold values from 0 to 13
- temps: float32 [14], replicated, may hold values from 0.7 to 1.5
- student_hidden: bfloat16 [256, 2048], P(None, 'variant'), may hold values from -24 to 24
- student_weight: bfloat16 [2048, 64128], P('variant', 'vocab'), may hold values from -1 to 1
- token_ids: int32 [256], P('variant'), may hold values from 0 to 64127
- loss_mask: int32 [256], P('variant'), may hold values 0 or 1
Outputs:
- token_loss: float32 [256], P('variant')
- student_grad: float32 [2048, 64128], P('variant', 'vocab')
All inputs are finite; a program needn't handle non-finite values. No bound on the sum of `loss_mask` on one device may be relied on, other than what follows from the above.
Results may differ from a plain program's by a relative error of at most 0.0025.
Values may be sent and summed in bfloat16 or wider, within the bound.
No kernel may reach another device: no remote copies, remote signals or barrier semaphores. Data moves between devices by JAX's collectives and lax.ppermute only.
A program may use at most 192 MiB of HBM per device.

v0:
```python
import jax
import jax.numpy as jnp
from jax import lax
from jax.sharding import PartitionSpec as P

mix_weight = 0.5
loss_scale = 4096.0


def on_device(
    teacher_hidden,
    teacher_weight,
    variant_ids,
    temps,
    student_hidden,
    student_weight,
    token_ids,
    loss_mask,
):
    n_variant = lax.axis_size("variant")
    categories = jnp.arange(temps.shape[0], dtype=jnp.int32)
    taus = jnp.sum(
        jnp.where(variant_ids[:, None] == categories[None, :], temps[None, :], 0.0), axis=1
    )
    hidden_all = lax.all_gather(teacher_hidden, ("variant", "vocab"), axis=2, tiled=True)
    scaled = (
        jnp.einsum("vtd,dc->vtc", hidden_all, teacher_weight, preferred_element_type=jnp.float32)
        / taus[:, None, None]
    )
    local_max = jnp.max(scaled, axis=2)
    top = lax.pmax(local_max, ("variant", "vocab"))
    total = lax.psum(jnp.sum(jnp.exp(scaled - top[:, :, None]), axis=2), ("variant", "vocab"))
    probs = jnp.exp(scaled - top[:, :, None]) / total[:, :, None]
    averaged_cols = jnp.sum(probs, axis=0) / n_variant
    averaged = lax.all_to_all(
        averaged_cols.astype(jnp.bfloat16), "variant", split_axis=0, concat_axis=1, tiled=True
    ).astype(averaged_cols.dtype)
    block = student_hidden
    logits = lax.psum_scatter(
        jnp.dot(block, student_weight, preferred_element_type=jnp.float32),
        "variant",
        scatter_dimension=0,
        tiled=True,
    )
    local_max = jnp.max(logits, axis=1)
    top = lax.pmax(local_max, "vocab")
    total = lax.psum(jnp.sum(jnp.exp(logits - top[:, None]), axis=1), "vocab")
    log_probs = logits - (top + jnp.log(total))[:, None]
    probs_student = jnp.exp(log_probs)
    columns = lax.axis_index("vocab") * logits.shape[1] + jnp.arange(
        logits.shape[1], dtype=jnp.int32
    )
    onehot = token_ids[:, None] == columns[None, :]
    soft, hard = lax.psum(
        (jnp.sum(averaged * log_probs, axis=1), jnp.sum(jnp.where(onehot, log_probs, 0.0), axis=1)),
        "vocab",
    )
    maskf = loss_mask.astype(jnp.float32)
    token_loss = maskf * (-mix_weight * soft - (1.0 - mix_weight) * hard)
    error = (
        loss_scale
        * maskf[:, None]
        * (probs_student - mix_weight * averaged - (1.0 - mix_weight) * onehot.astype(jnp.float32))
    ).astype(jnp.bfloat16)
    block = student_hidden
    student_grad = lax.dot_general(
        block,
        lax.all_gather(error, "variant", axis=0, tiled=True),
        (((0,), (0,)), ((), ())),
        preferred_element_type=jnp.float32,
    )
    return (token_loss, student_grad)


def solution(mesh):
    in_specs = (
        P(None, None, ("variant", "vocab")),
        P(None, ("vocab", "variant")),
        P(),
        P(),
        P(None, "variant"),
        P("variant", "vocab"),
        P("variant"),
        P("variant"),
    )
    out_specs = (P("variant"), P("variant", "vocab"))
    return jax.shard_map(
        on_device, mesh=mesh, in_specs=in_specs, out_specs=out_specs, check_vma=False
    )
```

profile of v0, /device:TPU:0, one launch (start us, length us, event | category | flops | bytes accessed | tf_op | source)
XLA Modules:
  0.0 505.8 jit_solution(16824957268856968234)
XLA Ops:
  8.0 0.0 copy-start
  8.0 0.0 reduce-scatter.2.cloned.1.call-start
  8.1 1.5 copy-done
  9.6 3.6 fusion.11
  13.2 0.0 reduce-scatter.2.cloned.1.call-update
  13.2 0.0 all-gather.3.cloned.1.call-start
  13.2 0.5 all-gather.3.cloned.1.call-update
  13.8 0.2 select_reduce_fusion
  14.0 60.6 %reduce-scatter.2.cloned.1.call-done = f32[32,4008]{1,0:T(8,128)} async-done(((f32[256,4008]{1,0:T(8,128)}), f32[32,4008]{1,0:T(8,128)}) %reduce-scatter.2.cloned.1.call-update) | async-done | bytes 513040 | tf_op jit(solution)/shard_map/reduce_scatter | solution.py:39
  74.6 1.2 reduce_max.19
  75.8 38.9 %pmax.15 = f32[32]{0:T(128)S(1)} all-reduce(f32[32]{0:T(128)S(1)} %reduce_max.19), channel_id=1, replica_groups=mesh['variant'=8,'vocab'=16] {'vocab'}, use_global_device_ids=true, to_apply=%region_8.9 | all-reduce | flops 32 | bytes 256 | tf_op jit(solution)/shard_map/pmax | solution.py:46
  114.7 151.1 %all-gather.3.cloned.1.call-done = bf16[8,256,4096]{1,2,0:T(8,128)(2,1)} async-done(((bf16[8,256,32]{1,2,0:T(8,128)(2,1)}), bf16[8,256,4096]{1,2,0:T(8,128)(2,1)}) %all-gather.3.cloned.1.call-update) | async-done | bytes 16777232 | tf_op jit(solution)/shard_map/all_gather | solution.py:25
  265.9 14.8 %fusion.10 = (f32[8,256]{1,0:T(8,128)S(1)}, f32[8,256,501]{1,2,0:T(8,128)}) fusion(f32[8]{0:T(128)S(1)} %select_reduce_fusion, bf16[8,256,4096]{1,2,0:T(8,128)(2,1)} %all-gather.3.cloned.1.call-done, bf16[4096,501]{0,1:T(8,128)(2,1)} %param.9), kind=kOutput, calls=%fused_computation.23 | convolution fusion | flops 8407435264 | bytes 24993824 | tf_op jit(solution)/shard_map/vtd,dc->vtc/dot_general | solution.py:27
  280.6 62.0 %pmax.14 = f32[8,256]{1,0:T(8,128)S(1)} all-reduce(f32[8,256]{1,0:T(8,128)S(1)} %get-tuple-element.7), channel_id=1, replica_groups=mesh['variant'=8,'vocab'=16] {'variant','vocab'}, use_global_device_ids=true, to_apply=%region_2.3 | all-reduce | flops 2048 | bytes 16384 | tf_op jit(solution)/shard_map/pmax | solution.py:31
  342.6 2.7 fusion.2
  345.4 64.6 %psum.28 = f32[8,256]{1,0:T(8,128)S(1)} all-reduce(f32[8,256]{1,0:T(8,128)S(1)} %fusion.2), channel_id=1, replica_groups=mesh['variant'=8,'vocab'=16] {'variant','vocab'}, use_global_device_ids=true, to_apply=%region_4.5 | all-reduce | flops 2048 | bytes 16384 | tf_op jit(solution)/shard_map/psum | solution.py:32
  410.0 2.9 divide_reduce_fusion
  412.9 0.0 copy-start.2
  413.0 0.8 copy.13
  413.8 3.4 all-to-all-start
  417.3 0.0 all-gather.5.cloned.1.call-start
  417.3 0.3 exponential_reduce_fusion
  417.6 34.1 %psum.29 = f32[32]{0:T(128)S(1)} all-reduce(f32[32]{0:T(128)S(1)} %exponential_reduce_fusion), channel_id=1, replica_groups=mesh['variant'=8,'vocab'=16] {'vocab'}, use_global_device_ids=true, to_apply=%region_10.11 | all-reduce | flops 32 | bytes 256 | tf_op jit(solution)/shard_map/psum | solution.py:47
  451.7 0.1 convert_bitcast_fusion
  451.8 1.1 copy.14
  452.9 1.4 reshape.27
  454.2 1.1 multiply_reduce_fusion
  455.4 0.0 all-gather.5.cloned.1.call-update
  455.4 33.7 %all-reduce = (f32[32]{0:T(128)S(1)}, f32[32]{0:T(128)S(1)}) all-reduce(f32[32]{0:T(128)S(1)} %get-tuple-element.3, f32[32]{0:T(128)S(1)} %get-tuple-element.2), channel_id=1, replica_groups=mesh['variant'=8,'vocab'=16] {'vocab'}, use_global_device_ids=true, to_apply=%region_14.15 | all-reduce | flops 64 | bytes 512 | tf_op jit(solution)/shard_map/psum | solution.py:54
  489.1 0.5 subtract_multiply_fusion
  489.6 4.4 all-gather.5.cloned.1.call-done
  494.0 4.3 convolution_bitcast_fusion
  (16 shorter events, 0.1 us)
Async XLA Ops:
  8.0 1.6 copy-start
  8.0 5.8 %copy-start.5 = (f32[14]{0:T(128)S(1)}, f32[14]{0:T(128)}, u32[]{:S(2)}) copy-start(f32[14]{0:T(128)} %param.11) | copy-start | bytes 172
  8.0 5.8 %copy-start.6 = (s32[8]{0:T(128)S(1)}, s32[8]{0:T(128)}, u32[]{:S(2)}) copy-start(s32[8]{0:T(128)} %param.10) | copy-start | bytes 100
  8.0 5.9 %copy-start.4 = (s32[32]{0:T(128)S(1)}, s32[32]{0:T(128)}, u32[]{:S(2)}) copy-start(s32[32]{0:T(128)} %param.15) | copy-start | bytes 388
  8.0 66.6 %reduce-scatter.2.cloned.1.call-start = ((), (), s32[]{:S(2)}) async-start(), calls=%async_computation.3 | async-start | bytes 4718592 | tf_op jit(solution)/shard_map/reduce_scatter | solution.py:39
  13.2 252.7 %all-gather.3.cloned.1.call-start = ((), (), s32[]{:S(2)}) async-start(), calls=%async_computation.2 | async-start | bytes 16908288 | tf_op jit(solution)/shard_map/all_gather | solution.py:25
  345.4 71.9 %copy-start.1 = (f32[32,4008]{1,0:T(8,128)S(1)}, f32[32,4008]{1,0:T(8,128)}, u32[]{:S(2)}) copy-start(f32[32,4008]{1,0:T(8,128)} %reduce-scatter.2.cloned.1.call-done) | copy-start | bytes 1539076
  410.0 44.2 %copy-start.3 = (s32[32]{0:T(128)S(1)}, s32[32]{0:T(128)}, u32[]{:S(2)}) copy-start(s32[32]{0:T(128)} %param.14) | copy-start | bytes 388
  412.9 81.1 %copy-start.2 = (bf16[256,256]{1,0:T(8,128)(2,1)S(1)}, bf16[256,256]{1,0:T(8,128)(2,1)}, u32[]{:S(2)}) copy-start(bf16[256,256]{1,0:T(8,128)(2,1)} %param.12) | copy-start | bytes 393220
  413.8 37.9 %all-to-all-start = ((bf16[8,32,501]{2,1,0:T(8,128)(2,1)}), bf16[8,32,501]{2,1,0:T(8,128)(2,1)S(1)}, u32[]{:S(2)}, u32[]{:S(2)}) async-start(bf16[8,32,501]{2,1,0:T(8,128)(2,1)} %bitcast.1), calls=%async_computation | async-start | bytes 524288 | tf_op jit(solution)/shard_map/all_to_all | solution.py:35
  417.3 76.8 %all-gather.5.cloned.1.call-start = ((), (), s32[]{:S(2)}) async-start(), calls=%async_computation.4 | async-start | bytes 2359296 | tf_op jit(solution)/shard_map/all_gather | solution.py:68
Sparse Core Ops, SparseCore 0:
  13.3 61.2 reduce-scatter.1
  455.5 38.4 all-gather.4
Sparse Core Ops, SparseCore 1:
  15.4 250.4 all-gather.2
where the time goes:
time: 506 us
  blocking collectives  233 us (46%)
  waiting for transfers between devices  217 us (43%)
  matrix products  22.7 us (4%)
  between operations  15.6 us (3%)
  other arithmetic  9.06 us (2%)
    all_gather x1, waiting for transfers between devices, on_device(): lax.all_gather(teacher_hidden, ('variant', 'vocab'), axis=2, tiled=True)  151 us
    psum x1, blocking collectives, on_device(): lax.psum(jnp.sum(jnp.exp(scaled - top[:, :, None]), axis=2), ('variant',...  64.6 us
    pmax x1, blocking collectives, on_device(): top = lax.pmax(local_max, ('variant', 'vocab'))  62 us
    reduce_scatter x1, waiting for transfers between devices, on_device(): lax.psum_scatter(jnp.dot(block, student_weight, preferred_element_type=jn...  60.6 us
    pmax x1, blocking collectives, on_device(): top = lax.pmax(local_max, 'vocab')  38.9 us
    psum x1, blocking collectives, on_device(): total = lax.psum(jnp.sum(jnp.exp(logits - top[:, None]), axis=1), 'vocab')  34.1 us
    psum x1, blocking collectives, on_device(): lax.psum((jnp.sum(averaged * log_probs, axis=1), jnp.sum(jnp.where(onehot...  33.7 us
    dot_general x1, matrix products, on_device(): jnp.einsum('vtd,dc->vtc', hidden_all, teacher_weight, preferred_element_t...  14.8 us
  transfers between devices with their start and end apart: 4, of which 3 were waited for; matrix products, arithmetic and copies ran while one was open for 0% of the time, Pallas kernels for 0%

commit v1 on v0

--- a/solution.py
+++ b/solution.py
@@ -22,7 +22,15 @@
     taus = jnp.sum(
         jnp.where(variant_ids[:, None] == categories[None, :], temps[None, :], 0.0), axis=1
     )
-    hidden_all = lax.all_gather(teacher_hidden, ("variant", "vocab"), axis=2, tiled=True)
+    hidden_all = jnp.concatenate(
+        lax.all_to_all(
+            jnp.stack([teacher_hidden] * lax.axis_size(("variant", "vocab"))),
+            ("variant", "vocab"),
+            0,
+            0,
+        ),
+        axis=2,
+    )
     scaled = (
         jnp.einsum("vtd,dc->vtc", hidden_all, teacher_weight, preferred_element_type=jnp.float32)
         / taus[:, None, None]

time: 506 us -> 545 us (1.077)
  blocking collectives: 233 us -> 303 us
  waiting for transfers between devices: 217 us -> 168 us
  local copies, waits for them, and re-layouts: 4.83 us -> 16.6 us
  starting transfers between devices: 3.54 us -> 15.3 us
    all_gather x1 -> x0, waiting for transfers between devices: 151 us -> none  [on_device(): lax.all_gather(teacher_hidden, ('variant', 'vocab'), axis=2, tiled=True)]
    reduce_scatter x1, waiting for transfers between devices: 60.6 us -> 162 us  [on_device(): lax.psum_scatter(jnp.dot(block, student_weight, preferred_element_type=jn...]
    pmax x1, blocking collectives: 38.9 us -> 92.1 us  [on_device(): top = lax.pmax(local_max, 'vocab')]
    pmax x1, blocking collectives: 62 us -> 78.7 us  [on_device(): top = lax.pmax(local_max, ('variant', 'vocab'))]
    all_to_all x0 -> x1, starting transfers between devices: none -> 11.7 us  [on_device(): lax.all_to_all(jnp.stack([teacher_hidden] * lax.axis_size(('variant', 'vo...]
    all_to_all x0 -> x1, local copies, waits for them, and re-layouts: none -> 8.22 us  [on_device(): lax.all_to_all(jnp.stack([teacher_hidden] * lax.axis_size(('variant', 'vo...]
    another operation x0 -> x1, local copies, waits for them, and re-layouts: none -> 6.86 us  [on_device(): jnp.stack([teacher_hidden] * lax.axis_size(('variant', 'vocab')))]
  transfers between devices with their start and end apart: 4 -> 4, of which waited for: 3 -> 3; matrix products, arithmetic and copies ran while one was open for 0% -> 1% of each run, Pallas kernels for 0% -> 0%
where the time goes in v1:
time: 545 us; the launch traced here: 544 us
  blocking collectives  303 us (56%)
  waiting for transfers between devices  168 us (31%)
  matrix products  19.1 us (4%)
  local copies, waits for them, and re-layouts  16.6 us (3%)
  starting transfers between devices  15.3 us (3%)
  between operations  14.2 us (3%)
  other arithmetic  9.01 us (2%)
    reduce_scatter x1, waiting for transfers between devices, on_device(): lax.psum_scatter(jnp.dot(block, student_weight, preferred_element_type=jn...  162 us
    pmax x1, blocking collectives, on_device(): top = lax.pmax(local_max, 'vocab')  92.1 us
    pmax x1, blocking collectives, on_device(): top = lax.pmax(local_max, ('variant', 'vocab'))  78.7 us
    psum x1, blocking collectives, on_device(): lax.psum(jnp.sum(jnp.exp(scaled - top[:, :, None]), axis=2), ('variant',...  62.7 us
    psum x1, blocking collectives, on_device(): total = lax.psum(jnp.sum(jnp.exp(logits - top[:, None]), axis=1), 'vocab')  35.3 us
    psum x1, blocking collectives, on_device(): lax.psum((jnp.sum(averaged * log_probs, axis=1), jnp.sum(jnp.where(onehot...  33.6 us
    dot_general x1, matrix products, on_device(): jnp.einsum('vtd,dc->vtc', hidden_all, teacher_weight, preferred_element_t...  12 us
    all_to_all x1, starting transfers between devices, on_device(): lax.all_to_all(jnp.stack([teacher_hidden] * lax.axis_size(('variant', 'vo...  11.7 us
  transfers between devices with their start and end apart: 4, of which 3 were waited for; matrix products, arithmetic and copies ran while one was open for 1% of the time, Pallas kernels for 0%

profile of v1, /device:TPU:0, one launch (start us, length us, event | category | flops | bytes accessed | tf_op | source)
XLA Modules:
  0.0 544.2 jit_solution(4545162584148173169)
XLA Ops:
  7.2 0.0 copy-start
  7.2 6.9 %stack.2 = bf16[128,8,256,32]{2,3,1,0:T(8,128)(2,1)} broadcast(bf16[8,256,32]{1,2,0:T(8,128)(2,1)} %param.8), dimensions={1,2,3} | broadcast | bytes 16908288 | tf_op jit(solution)/shard_map/stack | solution.py:27
  14.0 11.7 %all-to-all-start = ((bf16[128,8,256,32]{2,3,1,0:T(8,128)(2,1)}), bf16[128,8,256,32]{2,3,1,0:T(8,128)(2,1)}, u32[]{:S(2)}, u32[]{:S(2)}) async-start(bf16[128,8,256,32]{2,3,1,0:T(8,128)(2,1)} %stack.2), calls=%async_computation | async-start | bytes 33554432 | tf_op jit(solution)/shard_map/all_to_all | solution.py:26
  25.7 0.0 copy-start.7
  25.8 0.0 reduce-scatter.2.cloned.1.call-start
  25.8 2.8 fusion.11
  28.6 0.0 reduce-scatter.2.cloned.1.call-update
  28.7 0.2 select_reduce_fusion
  28.9 161.7 %reduce-scatter.2.cloned.1.call-done = f32[32,4008]{1,0:T(8,128)} async-done(((f32[256,4008]{1,0:T(8,128)}), f32[32,4008]{1,0:T(8,128)}) %reduce-scatter.2.cloned.1.call-update) | async-done | bytes 513040 | tf_op jit(solution)/shard_map/reduce_scatter | solution.py:47
  190.5 1.2 reduce_max.19
  191.7 92.1 %pmax.15 = f32[32]{0:T(128)S(1)} all-reduce(f32[32]{0:T(128)S(1)} %reduce_max.19), channel_id=1, replica_groups=mesh['variant'=8,'vocab'=16] {'vocab'}, use_global_device_ids=true, to_apply=%region_8.9 | all-reduce | flops 32 | bytes 256 | tf_op jit(solution)/shard_map/pmax | solution.py:54
  283.9 1.3 all-to-all-done
  285.2 8.2 %copy.17 = bf16[128,8,256,32]{2,3,0,1:T(8,128)(2,1)S(1)} copy(bf16[128,8,256,32]{2,3,1,0:T(8,128)(2,1)} %all-to-all-done) | data formatting | bytes 33554432 | tf_op jit(solution)/shard_map/all_to_all | solution.py:26
  293.4 12.0 %fusion.10 = (f32[8,256]{1,0:T(8,128)S(1)}, f32[8,256,501]{1,2,0:T(8,128)}) fusion(f32[8]{0:T(128)S(1)} %select_reduce_fusion, bf16[8,256,4096]{1,2,0:T(8,128)(2,1)S(1)} %bitcast.20, bf16[4096,501]{0,1:T(8,128)(2,1)} %param.9), kind=kOutput, calls=%fused_computation.23 | convolution fusion | flops 8407435264 | bytes 24993824 | tf_op jit(solution)/shard_map/vtd,dc->vtc/dot_general | solution.py:35
  305.4 78.7 %pmax.14 = f32[8,256]{1,0:T(8,128)S(1)} all-reduce(f32[8,256]{1,0:T(8,128)S(1)} %get-tuple-element.7), channel_id=1, replica_groups=mesh['variant'=8,'vocab'=16] {'variant','vocab'}, use_global_device_ids=true, to_apply=%region_2.3 | all-reduce | flops 2048 | bytes 16384 | tf_op jit(solution)/shard_map/pmax | solution.py:39
  384.1 2.7 fusion.2
  386.8 62.7 %psum.28 = f32[8,256]{1,0:T(8,128)S(1)} all-reduce(f32[8,256]{1,0:T(8,128)S(1)} %fusion.2), channel_id=1, replica_groups=mesh['variant'=8,'vocab'=16] {'variant','vocab'}, use_global_device_ids=true, to_apply=%region_4.5 | all-reduce | flops 2048 | bytes 16384 | tf_op jit(solution)/shard_map/psum | solution.py:40
  449.6 2.9 divide_reduce_fusion
  452.5 0.8 copy.19
  453.4 3.5 all-to-all-start.1
  456.9 0.0 all-gather.2.cloned.1.call-start
  457.0 0.3 exponential_reduce_fusion
  457.3 35.3 %psum.29 = f32[32]{0:T(128)S(1)} all-reduce(f32[32]{0:T(128)S(1)} %exponential_reduce_fusion), channel_id=1, replica_groups=mesh['variant'=8,'vocab'=16] {'vocab'}, use_global_device_ids=true, to_apply=%region_10.11 | all-reduce | flops 32 | bytes 256 | tf_op jit(solution)/shard_map/psum | solution.py:55
  492.6 0.1 convert_bitcast_fusion
  492.6 0.3 copy.20
  492.9 0.3 reshape.37
  493.3 1.1 multiply_reduce_fusion
  494.4 0.0 all-gather.2.cloned.1.call-update
  494.4 33.6 %all-reduce = (f32[32]{0:T(128)S(1)}, f32[32]{0:T(128)S(1)}) all-reduce(f32[32]{0:T(128)S(1)} %get-tuple-element.3, f32[32]{0:T(128)S(1)} %get-tuple-element.2), channel_id=1, replica_groups=mesh['variant'=8,'vocab'=16] {'vocab'}, use_global_device_ids=true, to_apply=%region_14.15 | all-reduce | flops 64 | bytes 512 | tf_op jit(solution)/shard_map/psum | solution.py:62
  528.1 0.5 subtract_multiply_fusion
  528.6 4.5 all-gather.2.cloned.1.call-done
  533.1 4.3 convolution_bitcast_fusion
  (19 shorter events, 0.1 us)
Async XLA Ops:
  7.2 18.7 %copy-start = (bf16[256,4008]{0,1:T(8,128)(2,1)S(1)}, bf16[256,4008]{0,1:T(8,128)(2,1)}, u32[]{:S(2)}) copy-start(bf16[256,4008]{0,1:T(8,128)(2,1)} %param.13) | copy-start | bytes 6156292
  14.0 11.8 %copy-start.3 = (bf16[256,256]{1,0:T(8,128)(2,1)S(1)}, bf16[256,256]{1,0:T(8,128)(2,1)}, u32[]{:S(2)}) copy-start(bf16[256,256]{1,0:T(8,128)(2,1)} %param.12) | copy-start | bytes 393220
  14.0 271.2 %all-to-all-start = ((bf16[128,8,256,32]{2,3,1,0:T(8,128)(2,1)}), bf16[128,8,256,32]{2,3,1,0:T(8,128)(2,1)}, u32[]{:S(2)}, u32[]{:S(2)}) async-start(bf16[128,8,256,32]{2,3,1,0:T(8,128)(2,1)} %stack.2), calls=%async_computation | async-start | bytes 33554432 | tf_op jit(solution)/shard_map/all_to_all | solution.py:26
  25.7 2.9 copy-start.6
  25.7 2.9 copy-start.7
  25.8 3.1 copy-start.5
  25.8 164.8 %reduce-scatter.2.cloned.1.call-start = ((), (), s32[]{:S(2)}) async-start(), calls=%async_computation.3 | async-start | bytes 4718592 | tf_op jit(solution)/shard_map/reduce_scatter | solution.py:47
  386.8 70.1 %copy-start.2 = (f32[32,4008]{1,0:T(8,128)S(1)}, f32[32,4008]{1,0:T(8,128)}, u32[]{:S(2)}) copy-start(f32[32,4008]{1,0:T(8,128)} %reduce-scatter.2.cloned.1.call-done) | copy-start | bytes 1539076
  449.6 43.7 %copy-start.4 = (s32[32]{0:T(128)S(1)}, s32[32]{0:T(128)}, u32[]{:S(2)}) copy-start(s32[32]{0:T(128)} %param.14) | copy-start | bytes 388
  453.4 39.2 %all-to-all-start.1 = ((bf16[8,32,501]{2,1,0:T(8,128)(2,1)}), bf16[8,32,501]{2,1,0:T(8,128)(2,1)S(1)}, u32[]{:S(2)}, u32[]{:S(2)}) async-start(bf16[8,32,501]{2,1,0:T(8,128)(2,1)} %bitcast.3), calls=%async_computation.1 | async-start | bytes 524288 | tf_op jit(solution)/shard_map/all_to_all | solution.py:43
  456.9 76.1 %all-gather.2.cloned.1.call-start = ((), (), s32[]{:S(2)}) async-start(), calls=%async_computation.4 | async-start | bytes 2359296 | tf_op jit(solution)/shard_map/all_gather | solution.py:76
  528.1 9.3 %copy-start.1 = (bf16[256,4008]{0,1:T(8,128)(2,1)S(1)}, bf16[256,4008]{0,1:T(8,128)(2,1)}, u32[]{:S(2)}) copy-start(bf16[256,4008]{0,1:T(8,128)(2,1)} %param.13) | copy-start | bytes 6156292
Sparse Core Ops, SparseCore 0:
  29.0 161.4 reduce-scatter.1
  494.5 38.4 all-gather.1
